TPU v7x, 32 devices: a whole 2x2x4 slice. The times are simulated.
32 devices in a mesh: groups: 1, rec: 32 (over z, y, x, core).
Axes of the slice: x: 2, y: 2, z: 4, core: 2. Of those that a mesh axis runs over, the one named last changes fastest.
Arguments:
- records: bfloat16 [4, 512, 2, 128], P(None, ('groups', 'rec')), may hold values from -6 to 6
- dest: int32 [512, 4], P('groups'), may hold values from 0 to 31, as said below
- w_in: bfloat16 [64, 36], replicated, may hold values from -1 to 1
- b_in: float32 [64], replicated, may hold values from -3 to 3
- w_mid: bfloat16 [64, 64], replicated, may hold values from -0.75 to 0.75
- b_mid: float32 [64], replicated, may hold values from -3 to 3
- w_out: bfloat16 [64, 36], replicated, may hold values from -0.25 to 0.25
Outputs:
- residual: float32 [4, 512, 2, 128], P(None, ('groups', 'rec'))
- grad_w_in: float32 [64, 36], P('groups')
- grad_b_in: float32 [64], P('groups')
- grad_w_mid: float32 [64, 64], P('groups')
- grad_b_mid: float32 [64], P('groups')
- grad_w_out: float32 [64, 36], P('groups')
Inputs may be any that keep to these rules, and one draw needn't show every extreme that they name: `dest`: from the 16 blocks of one record device at most 2 copies go to one owner; in every draw one owner receives exactly 2 copies from every record device.
All inputs are finite; a program needn't handle non-finite values.
Results may differ from a plain program's by a relative error of at most 0.0005.
The roundings to bfloat16 on the way count: a program that leaves them out, or rounds other values in their place, can miss the bound.
Values may be sent and summed in bfloat16 or wider, within the bound.
A program may use at most 192 MiB of HBM per device.

v0:
```python
import math

import jax
import jax.numpy as jnp
from jax import lax
from jax.sharding import PartitionSpec as P

VES = 4
CAP = 2


def patches(field, flip):
    count, height, width = field.shape
    padded = jnp.pad(field, ((0, 0), (1, 1), (1, 1)))
    taps = []
    for row in range(3):
        for col in range(3):
            top = 2 - row if flip else row
            left = 2 - col if flip else col
            taps.append(padded[:, top : top + height, left : left + width])
    return jnp.stack(taps, axis=1).reshape(count * 9, height, width)


def collect(terms, parts):
    height, width = (terms.shape[1], terms.shape[2])
    stacked = jnp.pad(terms.reshape(parts, 9, height, width), ((0, 0), (0, 0), (1, 1), (1, 1)))
    total = jnp.zeros((parts, height, width), jnp.float32)
    for row in range(3):
        for col in range(3):
            total = total + stacked[:, 3 * row + col, row : row + height, col : col + width]
    return total


def silu_grad(z):
    sig = jax.nn.sigmoid(z)
    return sig * (1.0 + z * (1.0 - sig))


def local(records, dest, w_in, b_in, w_mid, b_mid, w_out):
    count = lax.axis_size("rec")
    me = lax.axis_index("rec")
    parts, blocks, traces, samples = records.shape
    items = blocks * VES
    mine = lax.dynamic_slice_in_dim(dest, me * blocks, blocks, 0).reshape(items)
    owners = jnp.arange(count, dtype=jnp.int32)
    hits = (mine[:, None] == owners[None, :]).astype(jnp.int32)
    rank = jnp.sum((jnp.cumsum(hits, axis=0) - 1) * hits, axis=1)
    slot = mine * CAP + rank
    source = jnp.arange(items, dtype=jnp.int32) // VES

    def to_owners(field):
        outgoing = jnp.zeros((parts, count * CAP, traces, samples), jnp.bfloat16)
        outgoing = outgoing.at[:, slot].set(jnp.take(field, source, axis=1))
        arrived = lax.all_to_all(outgoing, "rec", split_axis=1, concat_axis=1, tiled=True)
        return arrived.reshape(parts, count * CAP * traces, samples)

    image = to_owners(records)
    inputs = patches(image, False)
    z1 = (
        jnp.einsum("cu,uhw->chw", w_in, inputs, preferred_element_type=jnp.float32)
        + b_in[:, None, None]
    )
    a1 = jax.nn.silu(z1).astype(jnp.bfloat16)
    z2 = (
        jnp.einsum("dc,chw->dhw", w_mid, a1, preferred_element_type=jnp.float32)
        + b_mid[:, None, None]
    )
    a2 = jax.nn.silu(z2).astype(jnp.bfloat16)
    terms = jnp.einsum("cu,chw->uhw", w_out, a2, preferred_element_type=jnp.float32)
    estimate = (
        collect(terms, parts).astype(jnp.bfloat16).reshape(parts, count * CAP, traces, samples)
    )
    returned = lax.all_to_all(estimate, "rec", split_axis=1, concat_axis=1, tiled=True)
    placed = jnp.take(returned, slot, axis=1).reshape(parts, blocks, VES, traces, samples)
    reblend = jnp.sum(placed, axis=2, dtype=jnp.float32)
    residual = reblend - records.astype(jnp.float32)
    grad_image = to_owners(residual.astype(jnp.bfloat16))
    scale = 1.0 / math.sqrt(parts * blocks * count * traces * samples)
    flipped = patches(grad_image, True)
    dw_out = jnp.einsum("chw,uhw->cu", a2, flipped, preferred_element_type=jnp.float32)
    da2 = jnp.einsum("cu,uhw->chw", w_out, flipped, preferred_element_type=jnp.float32)
    dz2 = (da2 * silu_grad(z2)).astype(jnp.bfloat16)
    dw_mid = jnp.einsum("dhw,chw->dc", dz2, a1, preferred_element_type=jnp.float32)
    db_mid = jnp.sum(dz2, axis=(1, 2), dtype=jnp.float32)
    da1 = jnp.einsum("dc,dhw->chw", w_mid, dz2, preferred_element_type=jnp.float32)
    dz1 = (da1 * silu_grad(z1)).astype(jnp.bfloat16)
    dw_in = jnp.einsum("chw,uhw->cu", dz1, inputs, preferred_element_type=jnp.float32)
    db_in = jnp.sum(dz1, axis=(1, 2), dtype=jnp.float32)
    total_in, total_bin, total_mid, total_bmid, total_out = lax.psum(
        (dw_in, db_in, dw_mid, db_mid, dw_out), "rec"
    )
    return (
        residual,
        total_in * scale,
        total_bin * scale,
        total_mid * scale,
        total_bmid * scale,
        total_out * scale,
    )


def solution(mesh):
    return jax.shard_map(
        local,
        mesh=mesh,
        in_specs=(
            P(None, ("groups", "rec"), None, None),
            P("groups", None),
            P(),
            P(),
            P(),
            P(),
            P(),
        ),
        out_specs=(
            P(None, ("groups", "rec"), None, None),
            P("groups", None),
            P("groups"),
            P("groups", None),
            P("groups"),
            P("groups", None),
        ),
        check_vma=False,
    )
```

profile of v0, /device:TPU:0, one launch (start us, length us, event | category | flops | bytes accessed | tf_op | source)
XLA Modules:
  0.0 121.9 jit_solution(512310915494927087)
XLA Ops:
  0.6 0.0 copy-start
  0.7 0.8 constant_dynamic-slice_fusion
  1.4 0.1 copy.68
  1.5 0.1 reshape.93
  1.6 0.1 fusion.68
  1.7 0.1 reduce_window_sum.11
  1.8 0.2 select_reduce_fusion
  2.0 0.1 mul.74
  2.1 0.6 pad_clamp_fusion.1
  2.7 1.8 %gather_fusion.1 = bf16[64,4,2,128]{3,2,1,0:T(2,128)(2,1)S(1)} fusion(bf16[4,16,2,128]{3,2,1,0:T(2,128)(2,1)} %param.9, s32[1024]{0:T(1024)} %pad_clamp_fusion.1), kind=kCustom, calls=%fused_computation.clone | custom fusion | bytes 262400 | tf_op jit(solution)/shard_map/jit(_take)/gather | solution.py:53
  4.5 0.2 broadcast_select_fusion.2
  4.7 0.0 copy-start.6
  4.8 2.5 %scatter_fusion = bf16[4,64,2,128]{3,0,2,1:T(4,128)(2,1)S(1)} fusion(bf16[4,64,2,128]{3,0,2,1:T(4,128)(2,1)S(1)} %broadcast.87.clone, s32[64]{0:T(128)S(1)} %fusion.75, bf16[64,4,2,128]{3,1,2,0:T(4,128)(2,1)S(1)} %copy.49), kind=kCustom, calls=%fused_computation.3 | custom fusion | bytes 393472 | tf_op jit(solution)/shard_map/scatter | solution.py:53
  7.3 15.3 %all_to_all.15 = bf16[4,64,2,128]{3,0,2,1:T(4,128)(2,1)S(1)} all-to-all(bf16[4,64,2,128]{3,0,2,1:T(4,128)(2,1)S(1)} %scatter_fusion), channel_id=1, replica_groups=mesh['groups'=1,'rec'=32] {'rec'}, dimensions={1} | all-to-all | bytes 262144 | tf_op jit(solution)/shard_map/all_to_all | solution.py:54
  22.6 0.1 fusion.37
  22.7 0.1 fusion.39
  22.8 0.1 fusion.41
  22.9 0.1 fusion.43
  23.1 0.1 fusion.45
  23.3 0.1 fusion.47
  23.4 0.1 fusion.49
  23.4 0.1 fusion.51
  23.6 0.1 copy.52
  23.7 0.0 copy-start.9
  23.7 3.7 %fusion.11 = (bf16[64,128,128]{2,0,1:T(8,128)(2,1)S(1)}, f32[128,128,64]{1,2,0:T(8,128)}) fusion(f32[64]{0:T(128)S(1)} %copy-done.11, bf16[64,36]{0,1:T(8,128)(2,1)S(1)} %copy-done.8, bf16[36,128,128]{2,1,0:T(8,128)(2,1)S(1)} %bitcast.178), kind=kOutput, calls=%fused_computation.32 | convolution fusion | flops 81788928 | bytes 7475968 | tf_op jit(solution)/shard_map/cu,uhw->chw/dot_general | solution.py:60
  27.4 3.4 %fusion.5 = (bf16[64,128,128]{2,0,1:T(8,128)(2,1)S(1)}, f32[128,128,64]{1,2,0:T(8,128)}) fusion(f32[64]{0:T(128)S(1)} %copy-done.9, bf16[64,128,128]{2,0,1:T(8,128)(2,1)S(1)} %get-tuple-element.20, bf16[64,64]{1,0:T(8,128)(2,1)S(1)} %copy-done), kind=kOutput, calls=%fused_computation.23 | convolution fusion | flops 140509184 | bytes 8397056 | tf_op jit(solution)/shard_map/dc,chw->dhw/dot_general | solution.py:65
  30.9 0.5 convolution_bitcast_fusion
  31.4 0.5 copy.54
  31.8 0.0 copy-start.3
  31.8 0.5 fusion.35
  32.3 0.7 copy.55
  33.1 2.6 %all-to-all-start.1 = ((bf16[4,64,2,128]{3,2,0,1:T(2,128)(2,1)}), bf16[4,64,2,128]{3,2,0,1:T(2,128)(2,1)S(1)}, u32[]{:S(2)}, u32[]{:S(2)}) async-start(bf16[4,64,2,128]{3,2,0,1:T(2,128)(2,1)} %copy.55), calls=%async_computation.1 | async-start | bytes 262144 | tf_op jit(solution)/shard_map/all_to_all | solution.py:73
  35.7 0.1 reduce_sum.41
  35.8 8.1 %all-to-all-done.1 = bf16[4,64,2,128]{3,2,0,1:T(2,128)(2,1)S(1)} async-done(((bf16[4,64,2,128]{3,2,0,1:T(2,128)(2,1)}), bf16[4,64,2,128]{3,2,0,1:T(2,128)(2,1)S(1)}, u32[]{:S(2)}, u32[]{:S(2)}) %all-to-all-start.1) | async-done | bytes 131104 | tf_op jit(solution)/shard_map/all_to_all | solution.py:73
  43.9 1.5 %gather_fusion = bf16[64,4,2,128]{3,2,1,0:T(2,128)(2,1)} fusion(bf16[4,64,2,128]{3,2,0,1:T(2,128)(2,1)S(1)} %all-to-all-done.1, s32[1024]{0:T(1024)S(1)} %pad_clamp_fusion), kind=kCustom, calls=%fused_computation.2 | custom fusion | bytes 262400 | tf_op jit(solution)/shard_map/jit(_take)/gather | solution.py:74
  45.3 1.2 convert_reduce_fusion.2
  46.6 1.0 gather_fusion.2
  47.6 0.9 broadcast_select_fusion.1
  48.5 0.7 broadcast.87
  49.2 7.5 %scatter_fusion.1 = bf16[4,64,2,128]{3,0,2,1:T(4,128)(2,1)} fusion(bf16[4,64,2,128]{3,0,2,1:T(4,128)(2,1)} %broadcast.87, s32[64]{0:T(128)} %copy-done.6, bf16[64,4,2,128]{3,1,2,0:T(4,128)(2,1)S(1)} %copy.57), kind=kCustom, calls=%fused_computation.4 | custom fusion | bytes 393472 | tf_op jit(solution)/shard_map/scatter | solution.py:53
  56.7 2.7 %all-to-all-start.2 = ((bf16[4,64,2,128]{3,0,2,1:T(4,128)(2,1)}), bf16[4,64,2,128]{3,0,2,1:T(4,128)(2,1)S(1)}, u32[]{:S(2)}, u32[]{:S(2)}) async-start(bf16[4,64,2,128]{3,0,2,1:T(4,128)(2,1)} %scatter_fusion.1), calls=%async_computation.2 | async-start | bytes 262144 | tf_op jit(solution)/shard_map/all_to_all | solution.py:54
  59.4 0.7 copy.65
  60.1 7.4 %all-to-all-done.2 = bf16[4,64,2,128]{3,0,2,1:T(4,128)(2,1)S(1)} async-done(((bf16[4,64,2,128]{3,0,2,1:T(4,128)(2,1)}), bf16[4,64,2,128]{3,0,2,1:T(4,128)(2,1)S(1)}, u32[]{:S(2)}, u32[]{:S(2)}) %all-to-all-start.2) | async-done | bytes 131104 | tf_op jit(solution)/shard_map/all_to_all | solution.py:54
  67.5 0.1 fusion.53
  67.6 0.1 fusion.55
  67.7 0.1 fusion.57
  67.8 0.1 fusion.59
  68.0 0.1 fusion.61
  68.1 0.1 fusion.63
  68.3 0.1 fusion.65
  68.3 0.1 fusion.67
  68.5 0.1 copy.60
  68.6 0.0 copy-start.5
  68.6 1.2 fusion.24
  69.7 0.9 copy-done.13
  70.7 4.3 %convert_reduce_fusion = (f32[64]{0:T(128)S(1)}, bf16[64,128,128]{2,0,1:T(8,128)(2,1)S(1)}) fusion(f32[128,128,64]{1,2,0:T(8,128)S(1)} %copy-done.13, f32[64]{0:T(128)S(1)} %copy-done.10, bf16[64,36]{0,1:T(8,128)(2,1)S(1)} %copy-done.5, bf16[36,128,128]{2,1,0:T(8,128)(2,1)S(1)} %bitcast.181), kind=kOutput, calls=%fused_computation.35 | convolution fusion | flops 88080320 | bytes 7476224 | tf_op jit(solution)/shard_map/cu,uhw->chw/dot_general | solution.py:81
  75.0 0.7 convolution_bitcast_fusion.1
  75.7 1.5 %copy-done.14 = f32[128,128,64]{1,2,0:T(8,128)S(1)} copy-done((f32[128,128,64]{1,2,0:T(8,128)S(1)}, f32[128,128,64]{1,2,0:T(8,128)}, u32[]{:S(2)}) %copy-start.14) | copy-done | bytes 4194328
  77.1 2.3 %convert_reduce_fusion.1 = (f32[64]{0:T(128)S(1)}, bf16[64,128,128]{2,0,1:T(8,128)(2,1)S(1)}) fusion(f32[128,128,64]{1,2,0:T(8,128)S(1)} %copy-done.14, f32[64]{0:T(128)S(1)} %copy-done.12, bf16[64,128,128]{2,0,1:T(8,128)(2,1)S(1)} %get-tuple-element.27, bf16[64,64]{1,0:T(8,128)(2,1)S(1)} %copy-done), kind=kOutput, calls=%fused_computation.36 | convolution fusion | flops 146800576 | bytes 8397312 | tf_op jit(solution)/shard_map/dc,dhw->chw/dot_general | solution.py:85
  79.4 1.2 fusion.21
  80.6 39.6 %all-reduce.3 = (f32[64,36]{0,1:T(8,128)S(1)}, f32[64]{0:T(128)S(1)}, f32[64,64]{1,0:T(8,128)S(1)}, f32[64]{0:T(128)S(1)}, f32[64,36]{0,1:T(8,128)S(1)}) all-reduce(f32[64,36]{0,1:T(8,128)S(1)} %fusion.21, f32[64]{0:T(128)S(1)} %get-tuple-element.24, ...), channel_id=1, replica_groups=mesh['groups'=1,'rec'=32] {'rec'}, use_global_device_ids=true, to_apply=%region_5.7 | all-reduce | flops 8832 | bytes 70656 | tf_op jit(solution)/shard_map/psum | solution.py:89
  120.2 0.6 broadcast_multiply_fusion
  120.8 0.6 broadcast_multiply_fusion.1
  121.4 0.5 broadcast_multiply_fusion.4
  (37 shorter events, 0.4 us)
Async XLA Ops:
  0.6 26.8 %copy-start = (bf16[64,64]{1,0:T(8,128)(2,1)S(1)}, bf16[64,64]{1,0:T(8,128)(2,1)}, u32[]{:S(2)}) copy-start(bf16[64,64]{1,0:T(8,128)(2,1)} %param.13) | copy-start | bytes 24580
  1.6 3.1 %copy-start.7 = (pred[64]{0:T(512)(128)(4,1)}, pred[64]{0:T(512)(128)(4,1)S(1)}, u32[]{:S(2)}) copy-start(pred[64]{0:T(512)(128)(4,1)S(1)} %compare_and_fusion.1) | copy-start | bytes 196
  4.7 30.9 %copy-start.6 = (s32[64]{0:T(128)}, s32[64]{0:T(128)S(1)}, u32[]{:S(2)}) copy-start(s32[64]{0:T(128)S(1)} %fusion.75) | copy-start | bytes 772
  22.8 0.9 copy-start.8
  22.8 0.9 copy-start.11
  23.7 3.7 %copy-start.9 = (f32[64]{0:T(128)S(1)}, f32[64]{0:T(128)}, u32[]{:S(2)}) copy-start(f32[64]{0:T(128)} %param.14) | copy-start | bytes 772
  27.4 3.4 %copy-start.1 = (bf16[64,128,128]{2,0,1:T(8,128)(2,1)}, bf16[64,128,128]{2,0,1:T(8,128)(2,1)S(1)}, u32[]{:S(2)}) copy-start(bf16[64,128,128]{2,0,1:T(8,128)(2,1)S(1)} %get-tuple-element.20) | copy-start | bytes 6291460
  27.4 3.4 %copy-start.4 = (bf16[64,36]{0,1:T(8,128)(2,1)S(1)}, bf16[64,36]{0,1:T(8,128)(2,1)}, u32[]{:S(2)}) copy-start(bf16[64,36]{0,1:T(8,128)(2,1)} %param.15) | copy-start | bytes 13828
  31.8 14.7 %copy-start.3 = (bf16[4,16,2,128]{3,2,1,0:T(2,128)(2,1)S(1)}, bf16[4,16,2,128]{3,2,1,0:T(2,128)(2,1)}, u32[]{:S(2)}) copy-start(bf16[4,16,2,128]{3,2,1,0:T(2,128)(2,1)} %param.9) | copy-start | bytes 98308
  33.1 10.8 %all-to-all-start.1 = ((bf16[4,64,2,128]{3,2,0,1:T(2,128)(2,1)}), bf16[4,64,2,128]{3,2,0,1:T(2,128)(2,1)S(1)}, u32[]{:S(2)}, u32[]{:S(2)}) async-start(bf16[4,64,2,128]{3,2,0,1:T(2,128)(2,1)} %copy.55), calls=%async_computation.1 | async-start | bytes 262144 | tf_op jit(solution)/shard_map/all_to_all | solution.py:73
  56.7 10.8 %all-to-all-start.2 = ((bf16[4,64,2,128]{3,0,2,1:T(4,128)(2,1)}), bf16[4,64,2,128]{3,0,2,1:T(4,128)(2,1)S(1)}, u32[]{:S(2)}, u32[]{:S(2)}) async-start(bf16[4,64,2,128]{3,0,2,1:T(4,128)(2,1)} %scatter_fusion.1), calls=%async_computation.2 | async-start | bytes 262144 | tf_op jit(solution)/shard_map/all_to_all | solution.py:54
  68.5 2.2 %copy-start.13 = (f32[128,128,64]{1,2,0:T(8,128)S(1)}, f32[128,128,64]{1,2,0:T(8,128)}, u32[]{:S(2)}) copy-start(f32[128,128,64]{1,2,0:T(8,128)} %get-tuple-element.23) | copy-start | bytes 12582916
  68.6 2.1 %copy-start.5 = (bf16[64,36]{0,1:T(8,128)(2,1)S(1)}, bf16[64,36]{0,1:T(8,128)(2,1)}, u32[]{:S(2)}) copy-start(bf16[64,36]{0,1:T(8,128)(2,1)} %param.15) | copy-start | bytes 13828
  68.6 2.1 %copy-start.10 = (f32[64]{0:T(128)S(1)}, f32[64]{0:T(128)}, u32[]{:S(2)}) copy-start(f32[64]{0:T(128)} %param.14) | copy-start | bytes 772
  70.7 4.3 %copy-start.2 = (bf16[64,128,128]{2,0,1:T(8,128)(2,1)S(1)}, bf16[64,128,128]{2,0,1:T(8,128)(2,1)}, u32[]{:S(2)}) copy-start(bf16[64,128,128]{2,0,1:T(8,128)(2,1)} %copy-done.1) | copy-start | bytes 6291460
  74.9 0.7 copy-start.12
  74.9 2.2 %copy-start.14 = (f32[128,128,64]{1,2,0:T(8,128)S(1)}, f32[128,128,64]{1,2,0:T(8,128)}, u32[]{:S(2)}) copy-start(f32[128,128,64]{1,2,0:T(8,128)} %get-tuple-element.21) | copy-start | bytes 12582916
where the time goes:
time: 123 us; the launch traced here: 122 us
  blocking collectives  54.9 us (45%)
  local copies, waits for them, and re-layouts  22.5 us (18%)
  matrix products  17.1 us (14%)
  waiting for transfers between devices  15.5 us (13%)
  other arithmetic  5.52 us (4%)
  starting transfers between devices  5.3 us (4%)
    psum x1, blocking collectives, local(): lax.psum((dw_in, db_in, dw_mid, db_mid, dw_out), 'rec')  39.6 us
    all_to_all x1, blocking collectives, to_owners(): lax.all_to_all(outgoing, 'rec', split_axis=1, concat_axis=1, tiled=True)  15.3 us
    scatter x2, local copies, waits for them, and re-layouts, to_owners(): outgoing = outgoing.at[:, slot].set(jnp.take(field, source, axis=1))  9.96 us
    all_to_all x1, waiting for transfers between devices, local(): lax.all_to_all(estimate, 'rec', split_axis=1, concat_axis=1, tiled=True)  8.11 us
    all_to_all x1, waiting for transfers between devices, to_owners(): lax.all_to_all(outgoing, 'rec', split_axis=1, concat_axis=1, tiled=True)  7.39 us
    unnamed x48, local copies, waits for them, and re-layouts  4.76 us
    dot_general x1, matrix products, local(): jnp.einsum('cu,uhw->chw', w_out, flipped, preferred_element_type=jnp.floa...  4.26 us
    dot_general x1, matrix products, local(): jnp.einsum('cu,uhw->chw', w_in, inputs, preferred_element_type=jnp.float32)  3.69 us
  transfers between devices with their start and end apart: 2, of which 2 were waited for; matrix products, arithmetic and copies ran while one was open for 1% of the time, Pallas kernels for 0%

commit v1 on v0

v1 whole, which is shorter than its diff:
```python
import functools
import math

import jax
import jax.numpy as jnp
from jax import lax
from jax.experimental import pallas as pl
from jax.experimental.pallas import tpu as pltpu
from jax.sharding import PartitionSpec as P

VES = 4
CAP = 2
F32 = jnp.float32
BF16 = jnp.bfloat16
NT = (((1,), (1,)), ((), ()))


def iota(shape, dim):
    return lax.broadcasted_iota(jnp.int32, shape, dim)


def dot(a, b, dims=None):
    if dims is None:
        return jnp.dot(a, b, preferred_element_type=F32)
    return lax.dot_general(a, b, dims, preferred_element_type=F32)


def onehot(mask):
    return jnp.where(mask, 1.0, 0.0).astype(F32)


def tap_of(k, q_out, flip):
    tile, col, trace, comp = k // 64, (k // 16) % 4, (k // 4) % 4, k % 4
    row = 4 * (tile - 1) + trace - q_out + 1
    ok = (row >= 0) & (row <= 2) & (col <= 2) & (tile <= 2)
    if flip:
        row, col = 2 - row, 2 - col
    return jnp.where(ok, 9 * comp + 3 * row + col, -1)


def kernel(
    n, scale, chunk,
    rec_ref, dest_ref, w_in_ref, b_in_ref, w_mid_ref, b_mid_ref, w_out_ref,
    res_ref, grad_ref,
    mine, out1, in1, est, in2, out3, in3, parts, in4, part, in5,
    sel, sel_t, wt1, wt2, wt2_t, wm, wm_t, bias1, bias2,
    xs, qs, acc, a1s, a2s, d1s, d2s, g1, g2, gm, gb,
    dest_sem, send_sem, recv_sem,
):
    me = lax.axis_index("rec")
    blocks = mine.shape[0]

    barrier = pltpu.get_barrier_semaphore()

    def greet(d, _):
        pl.semaphore_signal(
            barrier, inc=1, device_id={"rec": (me + d) % n}, device_id_type=pl.DeviceIdType.MESH
        )
        return 0

    fetch = pltpu.make_async_copy(
        dest_ref.at[pl.ds(pl.multiple_of(me * blocks, blocks), blocks)], mine, dest_sem
    )
    fetch.start()
    lax.fori_loop(1, n, greet, 0)

    def exchange(src, dst, phase):
        def send(d, _):
            peer = (me + d) % n
            pltpu.make_async_remote_copy(
                src_ref=src.at[peer],
                dst_ref=dst.at[me],
                send_sem=send_sem.at[phase],
                recv_sem=recv_sem.at[phase],
                device_id={"rec": peer},
                device_id_type=pl.DeviceIdType.MESH,
            ).start()
            return 0

        lax.fori_loop(1, n, send, 0)
        dst[me] = src[me]

    def arrive(dst, phase):
        whole = dst.at[pl.ds(0, n - 1)]
        pltpu.make_async_copy(whole, whole, recv_sem.at[phase]).wait()

    def sent(src, phase):
        whole = src.at[pl.ds(0, n - 1)]
        pltpu.make_async_copy(whole, whole, send_sem.at[phase]).wait()

    fetch.wait()
    column = iota((blocks, 128), 1)
    item = (column // 2) % blocks
    block = iota((blocks, 128), 0)
    here = [jnp.broadcast_to(mine[:, v : v + 1], (blocks, 128)) for v in range(VES)]
    lane = iota((1, 128), 1)
    inner = (lane % 2) * 4 + lane // 32
    rows = iota((16 * n, 128), 0)
    mask = None
    for v in range(VES):
        own = jnp.sum(jnp.where(block == item, here[v], 0), axis=0, keepdims=True)
        rank = jnp.zeros((blocks, 128), jnp.int32)
        for u in range(VES):
            before = (block <= item) if u < v else (block < item)
            rank = rank + jnp.where(before & (here[u] == own), 1, 0)
        target = (own * CAP + jnp.sum(rank, axis=0, keepdims=True)) * 8 + inner
        hit = rows == target
        mask = hit if mask is None else mask | hit
    picked = onehot(mask)
    sel[...] = picked.astype(BF16)
    out1[...] = dot(sel[...], rec_ref[...]).astype(BF16).reshape(n, 16, 128)
    pl.semaphore_wait(barrier, n - 1)
    exchange(out1, in1, 0)

    sel_t[...] = picked.T.astype(BF16)
    u = iota((36, 256), 0)
    k = iota((36, 256), 1)
    for q in range(4):
        span = slice(64 * q, 64 * q + 64)
        wt1[span] = dot(w_in_ref[...], onehot(u == tap_of(k, q, False)).astype(BF16)).astype(BF16)
        wt2[span] = dot(w_out_ref[...], onehot(u == tap_of(k, q, True)).astype(BF16)).astype(BF16)
    wt2_t[...] = wt2[...].astype(F32).T.astype(BF16)
    tall = onehot(iota((256, 64), 0) % 64 == iota((256, 64), 1)).astype(BF16)
    wide = onehot(iota((64, 256), 1) % 64 == iota((64, 256), 0)).astype(BF16)
    diagonal = iota((256, 256), 0) // 64 == iota((256, 256), 1) // 64
    once = dot(dot(tall, w_mid_ref[...]).astype(BF16), wide)
    once = jnp.where(diagonal, once, 0.0)
    wm[...] = once.astype(BF16)
    wm_t[...] = once.T.astype(BF16)
    near = iota((256, 64), 0) % 64 == iota((256, 64), 1)
    for b_ref, bias in ((b_in_ref, bias1), (b_mid_ref, bias2)):
        values = jnp.sum(jnp.where(near, b_ref[...], 0.0), axis=1, keepdims=True)
        bias[...] = jnp.broadcast_to(values, (256, 128))
    right = iota((128, 256), 1)
    left = iota((128, 256), 0)
    shift = onehot(
        ((right < 128) & (left == right - 1)) | ((right >= 128) & (left == right - 127))
    ).astype(BF16)
    for field in (xs, qs):
        field[:, 0:128] = jnp.zeros((64, 128), BF16)
        field[:, (n + 1) * 128 :] = jnp.zeros((64, 128), BF16)
        field[48:64, :] = onehot(iota((16, (n + 2) * 128), 0) == 0).astype(BF16)
    acc[...] = jnp.zeros_like(acc)
    for g in (g1, g2, gm, gb):
        g[...] = jnp.zeros_like(g)

    def spread(src, field):
        def step(c, _):
            tiles = src[pl.ds(c * 8, 8)].reshape(128, 128)
            moved = dot(tiles, shift).astype(BF16)
            for t in range(8):
                at = pl.ds(pl.multiple_of((c * 8 + t + 1) * 128, 128), 128)
                span = slice(16 * t, 16 * t + 16)
                field[0:16, at] = moved[span, 0:128]
                field[16:32, at] = tiles[span]
                field[32:48, at] = moved[span, 128:256]
            return 0

        lax.fori_loop(0, n // 8, step, 0)

    size = chunk * 128

    def stack(field, c):
        parts_ = [
            field[:, pl.ds(pl.multiple_of(c * size + d * 128, 128), size)] for d in range(3)
        ]
        return jnp.concatenate(parts_ + [jnp.zeros((64, size), BF16)], axis=0)

    def activate(z, a, d, at):
        s = 0.5 * jnp.tanh(0.5 * z) + 0.5
        out = (z * s).astype(BF16)
        a[:, at] = out
        d[:, at] = s * (1.0 + z * (1.0 - s))
        return out

    arrive(in1, 0)
    spread(in1, xs)

    def forward(c, _):
        at = pl.ds(pl.multiple_of(c * size, 128), size)
        b1 = jnp.concatenate([bias1[...]] * chunk, axis=1)
        b2 = jnp.concatenate([bias2[...]] * chunk, axis=1)
        a1 = activate(dot(wt1[...], stack(xs, c)) + b1, a1s, d1s, at)
        a2 = activate(dot(wm[...], a1) + b2, a2s, d2s, at)
        terms = dot(wt2_t[...], a2)
        for d in range(3):
            to = pl.ds(pl.multiple_of(c * size + d * 128, 128), size)
            acc[:, to] = acc[:, to] + terms[64 * d : 64 * d + 48]
        return 0

    lax.fori_loop(0, n // chunk, forward, 0)

    sample = iota((16, 128), 1)

    def close(s, _):
        at = pl.ds(pl.multiple_of((s + 1) * 128, 128), 128)
        before = jnp.where(sample < 127, pltpu.roll(acc[0:16, at], 127, 1), 0.0)
        after = jnp.where(sample > 0, pltpu.roll(acc[32:48, at], 1, 1), 0.0)
        est[s] = (acc[16:32, at] + before + after).astype(BF16)
        return 0

    lax.fori_loop(0, n, close, 0)
    exchange(est, in2, 1)
    arrive(in2, 1)
    residual = dot(sel_t[...], in2[...].reshape(16 * n, 128)) - rec_ref[...].astype(F32)
    res_ref[...] = residual
    out3[...] = dot(sel[...], residual.astype(BF16)).astype(BF16).reshape(n, 16, 128)
    exchange(out3, in3, 2)
    arrive(in3, 2)
    spread(in3, qs)

    def backward(c, _):
        at = pl.ds(pl.multiple_of(c * size, 128), size)
        field = stack(qs, c)
        g2[...] += dot(a2s[:, at], field, NT)
        dz2 = dot(wt2[...], field) * d2s[:, at]
        dz2 = dz2.astype(BF16)
        for t in range(chunk):
            gb[...] += dz2[:, 128 * t : 128 * t + 128].astype(F32)
        gm[...] += dot(dz2, a1s[:, at], NT)
        dz1 = (dot(wm_t[...], dz2) * d1s[:, at]).astype(BF16)
        g1[...] += dot(dz1, stack(xs, c), NT)
        return 0

    lax.fori_loop(0, n // chunk, backward, 0)

    lane = iota((64, 128), 1)
    deep = iota((256, 128), 0)
    across = iota((256, 128), 1)
    first = jnp.zeros((64, 128), F32)
    for q in range(4):
        span = slice(64 * q, 64 * q + 64)
        for g, fold in (
            (g1, (across == tap_of(deep, q, False)) | ((deep == 112) & (across == 36))),
            (g2, across - 64 == jnp.where(tap_of(deep, q, True) < 0, -100, tap_of(deep, q, True))),
        ):
            x = g[span]
            high = x.astype(BF16)
            rest = x - high.astype(F32)
            middle = rest.astype(BF16)
            low = (rest - middle.astype(F32)).astype(BF16)
            three = dot(jnp.concatenate([high, middle, low], axis=0), onehot(fold).astype(BF16))
            first = first + (three[0:64] + three[64:128] + three[128:192])
    square = jnp.where(diagonal, gm[...], 0.0)
    square = square[0:64] + square[64:128] + square[128:192] + square[192:256]
    square = square[:, 0:128] + square[:, 128:256]
    square = square + pltpu.roll(square, 64, 1)
    summed = jnp.sum(gb[...], axis=1, keepdims=True)
    summed = summed[0:64] + summed[64:128] + summed[128:192] + summed[192:256]
    second = jnp.where(lane < 64, square, jnp.where(lane == 64, summed, 0.0))
    per = 128 // n
    for i in range(n):
        source = first if i * per < 64 else second
        start = (i * per) % 64
        parts[i] = source[start : start + per]

    exchange(parts, in4, 3)
    arrive(in4, 3)
    part[...] = jnp.sum(in4[...], axis=0, keepdims=True) * scale

    def share(d, _):
        peer = (me + d) % n
        pltpu.make_async_remote_copy(
            src_ref=part.at[0],
            dst_ref=in5.at[me],
            send_sem=send_sem.at[4],
            recv_sem=recv_sem.at[4],
            device_id={"rec": peer},
            device_id_type=pl.DeviceIdType.MESH,
        ).start()
        return 0

    lax.fori_loop(1, n, share, 0)
    in5[me] = part[0]
    arrive(in5, 4)
    for i in range(n):
        grad_ref[per * i : per * i + per] = in5[i]
    sent(out1, 0)
    sent(est, 1)
    sent(out3, 2)
    sent(parts, 3)
    sent(in5, 4)


def local(n, records, dest, w_in, b_in, w_mid, b_mid, w_out):
    parts, blocks, traces, samples = records.shape
    width = n * samples
    per = 128 // n
    chunk = 4
    scale = 1.0 / math.sqrt(parts * blocks * n * traces * samples)
    vmem = pl.BlockSpec(memory_space=pltpu.VMEM)
    V = pltpu.VMEM
    message = V((n, 16, 128), BF16)
    piece = V((n, per, 128), F32)
    residual, grads = pl.pallas_call(
        functools.partial(kernel, n, scale, chunk),
        out_shape=(
            jax.ShapeDtypeStruct((128, 128), F32),
            jax.ShapeDtypeStruct((128, 128), F32),
        ),
        in_specs=[vmem, pl.BlockSpec(memory_space=pl.ANY)] + [vmem] * 5,
        out_specs=(vmem, vmem),
        scratch_shapes=[
            V((blocks, VES), jnp.int32),
            message, message, message, message, message, message,
            piece, piece, V((1, per, 128), F32), piece,
            V((16 * n, 128), BF16), V((128, 16 * n), BF16),
            V((256, 256), BF16), V((256, 256), BF16), V((256, 256), BF16),
            V((256, 256), BF16), V((256, 256), BF16),
            V((256, 128), F32), V((256, 128), F32),
            V((64, width + 256), BF16), V((64, width + 256), BF16), V((48, width + 256), F32),
            V((256, width), BF16), V((256, width), BF16), V((256, width), F32), V((256, width), F32),
            V((256, 256), F32), V((256, 256), F32), V((256, 256), F32), V((256, 128), F32),
            pltpu.SemaphoreType.DMA, pltpu.SemaphoreType.DMA((5,)), pltpu.SemaphoreType.DMA((5,)),
        ],
        compiler_params=pltpu.CompilerParams(
            collective_id=0, has_side_effects=True, vmem_limit_bytes=63 * 1024 * 1024
        ),
        name="deblend",
    )(
        records.reshape(128, 128), dest, w_in, b_in.reshape(1, 64), w_mid, b_mid.reshape(1, 64), w_out
    )
    return (
        residual.reshape(records.shape),
        grads[0:64, 0:36],
        grads[0:64, 36],
        grads[64:128, 0:64],
        grads[64:128, 64],
        grads[0:64, 64:100],
    )


def solution(mesh):
    return jax.shard_map(
        functools.partial(local, mesh.shape["rec"]),
        mesh=mesh,
        in_specs=(
            P(None, ("groups", "rec"), None, None),
            P("groups", None),
            P(),
            P(),
            P(),
            P(),
            P(),
        ),
        out_specs=(
            P(None, ("groups", "rec"), None, None),
            P("groups", None),
            P("groups"),
            P("groups", None),
            P("groups"),
            P("groups", None),
        ),
        check_vma=False,
    )
```

time: 123 us -> 58.2 us (0.47)
  blocking collectives: 54.9 us -> 0 us
  Pallas kernels: 0 us -> 49.9 us
  matrix products: 17.1 us -> 0 us
  waiting for transfers between devices: 15.5 us -> 0 us
  local copies, waits for them, and re-layouts: 22.5 us -> 7.2 us
  other arithmetic: 5.52 us -> 0 us
  starting transfers between devices: 5.3 us -> 0 us
    pallas_call x0 -> x1, Pallas kernels: none -> 49.9 us  [local(): pl.pallas_call(functools.partial(kernel, n, scale, chunk), out_shape=(jax...]
    psum x1 -> x0, blocking collectives: 39.6 us -> none  [local(): lax.psum((dw_in, db_in, dw_mid, db_mid, dw_out), 'rec')]
    dot_general x8 -> x0, matrix products: 17.1 us -> none  [the longest x1 4.26 us: local(): jnp.einsum('cu,uhw->chw', w_out, flipped, preferred_element_type=jnp.floa...]
    all_to_all x2 -> x0, waiting for transfers between devices: 15.5 us -> none  [the longest x1 8.11 us: local(): lax.all_to_all(estimate, 'rec', split_axis=1, concat_axis=1, tiled=True)]
    all_to_all x1 -> x0, blocking collectives: 15.3 us -> none  [to_owners(): lax.all_to_all(outgoing, 'rec', split_axis=1, concat_axis=1, tiled=True)]
    scatter x2 -> x0, local copies, waits for them, and re-layouts: 9.96 us -> none  [to_owners(): outgoing = outgoing.at[:, slot].set(jnp.take(field, source, axis=1))]
    all_to_all x2 -> x0, starting transfers between devices: 5.3 us -> none  [the longest x1 2.74 us: to_owners(): lax.all_to_all(outgoing, 'rec', split_axis=1, concat_axis=1, tiled=True)]
    gather x3 -> x0, local copies, waits for them, and re-layouts: 4.22 us -> none  [the longest x2 2.74 us: to_owners(): outgoing = outgoing.at[:, slot].set(jnp.take(field, source, axis=1))]
  transfers between devices with their start and end apart: 2 -> 0, of which waited for: 2 -> 0; matrix products, arithmetic and copies ran while one was open for 1% -> 0% of each run, Pallas kernels for 0% -> 0%
where the time goes in v1:
time: 58.2 us; the launch traced here: 57.7 us
  Pallas kernels  49.9 us (86%)
  local copies, waits for them, and re-layouts  7.2 us (12%)
  between operations  0.66 us (1%)
    pallas_call x1, Pallas kernels, local(): pl.pallas_call(functools.partial(kernel, n, scale, chunk), out_shape=(jax...  49.9 us
    unnamed x14, local copies, waits for them, and re-layouts  4.97 us
    slice x1, local copies, waits for them, and re-layouts, local(): grads[64:128, 64]  1.53 us

profile of v1, /device:TPU:0, one launch (start us, length us, event | category | flops | bytes accessed | tf_op | source)
XLA Modules:
  0.0 57.7 jit_solution(473027340423560209)
XLA Ops:
  0.6 0.0 copy-start.2
  0.6 1.4 %copy.19.w_in_ref = bf16[64,36]{1,0:T(8,128)(2,1)} copy(bf16[64,36]{0,1:T(8,128)(2,1)} %param.9) | data formatting | bytes 9216 | tf_op args[2]
  2.0 0.0 copy-done.2
  2.0 0.0 copy-start.3
  2.0 0.7 %copy.20.w_out_ref = bf16[64,36]{1,0:T(8,128)(2,1)} copy(bf16[64,36]{0,1:T(8,128)(2,1)S(1)} %copy-done.2) | data formatting | bytes 9216 | tf_op args[6]
  2.7 0.0 copy-done.3
  2.8 0.8 %copy.18.dest_ref = s32[512,4]{1,0:T(8,128)} copy(s32[512,4]{0,1:T(4,128)S(1)} %copy-done.3) | data formatting | bytes 16384 | tf_op args[1]
  3.6 49.9 %deblend.1 = (f32[128,128]{1,0:T(8,128)}, f32[128,128]{1,0:T(8,128)}) custom-call(bf16[128,128]{1,0:T(8,128)(2,1)} %bitcast.5, s32[512,4]{1,0:T(8,128)} %copy.18.dest_ref, bf16[64,36]{1,0:T(8,128)(2,1)} %copy.19.w_in_ref, f32[1,64]{1,0:T(1,128)} %bitcast.6, bf16[64,64]{1,0:T(8,128)(2,1)} %w_mid_ref.1, f32[1,64]{1,0:T(1,128)} %bitcast.7, ...), custom_call_target="tpu_custom_call" | custom-call | tf_op jit(solution)/shard_map/deblend/pallas_call | solution.py:295
  53.5 0.0 copy-start
  53.5 1.5 %slice_reduce_fusion = (f32[64]{0:T(128)}, f32[64]{0:T(128)}) fusion(f32[128,128]{1,0:T(8,128)} %get-tuple-element.9), kind=kLoop, calls=%fused_computation | loop fusion | bytes 1024 | tf_op jit(solution)/shard_map/slice | solution.py:328
  55.0 0.0 copy-done
  55.0 0.6 %slice.17 = f32[64,64]{1,0:T(8,128)} slice(f32[128,128]{1,0:T(8,128)S(1)} %copy-done), slice={[64:128], [0:64]} | slice | bytes 32768 | tf_op jit(solution)/shard_map/slice | solution.py:327
  55.6 0.1 fusion
  55.7 0.0 copy-start.1
  55.7 0.7 %copy.22 = f32[64,36]{0,1:T(8,128)} copy(f32[64,36]{1,0:T(8,128)S(1)} %get-tuple-element.24) | data formatting | bytes 18432
  56.4 0.7 %copy.21 = f32[64,36]{0,1:T(8,128)} copy(f32[64,36]{1,0:T(8,128)S(1)} %get-tuple-element.25) | data formatting | bytes 18432
  57.1 0.0 copy-done.1
  57.1 0.6 %copy.24 = f32[4,16,2,128]{3,2,1,0:T(2,128)} copy(f32[4,16,2,128]{3,2,1,0:T(2,128)S(1)} %bitcast.4) | data formatting | bytes 131072
Async XLA Ops:
  0.6 1.4 %copy-start.2 = (bf16[64,36]{0,1:T(8,128)(2,1)S(1)}, bf16[64,36]{0,1:T(8,128)(2,1)}, u32[]{:S(2)}) copy-start(bf16[64,36]{0,1:T(8,128)(2,1)} %param.13) | copy-start | bytes 13828
  2.0 0.7 %copy-start.3 = (s32[512,4]{0,1:T(4,128)S(1)}, s32[512,4]{0,1:T(4,128)}, u32[]{:S(2)}) copy-start(s32[512,4]{0,1:T(4,128)} %param.8) | copy-start | bytes 24580
  53.5 1.5 %copy-start = (f32[128,128]{1,0:T(8,128)S(1)}, f32[128,128]{1,0:T(8,128)}, u32[]{:S(2)}) copy-start(f32[128,128]{1,0:T(8,128)} %get-tuple-element.9) | copy-start | bytes 196612
  55.7 1.4 %copy-start.1 = (f32[128,128]{1,0:T(8,128)S(1)}, f32[128,128]{1,0:T(8,128)}, u32[]{:S(2)}) copy-start(f32[128,128]{1,0:T(8,128)} %get-tuple-element.8) | copy-start | bytes 196612

commit v2 on v1

--- a/solution.py
+++ b/solution.py
@@ -13,6 +13,7 @@
 F32 = jnp.float32
 BF16 = jnp.bfloat16
 NT = (((1,), (1,)), ((), ()))
+TN = (((0,), (0,)), ((), ()))
 
 
 def iota(shape, dim):
@@ -30,7 +31,7 @@
 
 
 def tap_of(k, q_out, flip):
-    tile, col, trace, comp = k // 64, (k // 16) % 4, (k // 4) % 4, k % 4
+    tile, col, trace, comp = k >> 6, (k >> 4) & 3, (k >> 2) & 3, k & 3
     row = 4 * (tile - 1) + trace - q_out + 1
     ok = (row >= 0) & (row <= 2) & (col <= 2) & (tile <= 2)
     if flip:
@@ -42,13 +43,13 @@
     n, scale, chunk,
     rec_ref, dest_ref, w_in_ref, b_in_ref, w_mid_ref, b_mid_ref, w_out_ref,
     res_ref, grad_ref,
-    mine, out1, in1, est, in2, out3, in3, parts, in4, part, in5,
+    out1, in1, est, in2, out3, in3, parts, in4, part, in5,
     sel, sel_t, wt1, wt2, wt2_t, wm, wm_t, bias1, bias2,
-    xs, qs, acc, a1s, a2s, d1s, d2s, g1, g2, gm, gb,
-    dest_sem, send_sem, recv_sem,
+    xs, qs, acc, a1s, a2s, d1s, d2s, g1, g2, gm, gb, fold1, fold2,
+    send_sem, recv_sem,
 ):
     me = lax.axis_index("rec")
-    blocks = mine.shape[0]
+    blocks = rec_ref.shape[0] // 8
 
     barrier = pltpu.get_barrier_semaphore()
 
@@ -58,11 +59,7 @@
         )
         return 0
 
-    fetch = pltpu.make_async_copy(
-        dest_ref.at[pl.ds(pl.multiple_of(me * blocks, blocks), blocks)], mine, dest_sem
-    )
-    fetch.start()
-    lax.fori_loop(1, n, greet, 0)
+    lax.fori_loop(1, n, greet, 0, unroll=True)
 
     def exchange(src, dst, phase):
         def send(d, _):
@@ -77,24 +74,30 @@
             ).start()
             return 0
 
-        lax.fori_loop(1, n, send, 0)
+        lax.fori_loop(1, n, send, 0, unroll=True)
         dst[me] = src[me]
 
     def arrive(dst, phase):
-        whole = dst.at[pl.ds(0, n - 1)]
-        pltpu.make_async_copy(whole, whole, recv_sem.at[phase]).wait()
+        every = dst.at[pl.ds(0, n - 1)]
+        pltpu.make_async_copy(every, every, recv_sem.at[phase]).wait()
 
     def sent(src, phase):
-        whole = src.at[pl.ds(0, n - 1)]
-        pltpu.make_async_copy(whole, whole, send_sem.at[phase]).wait()
-
-    fetch.wait()
+        every = src.at[pl.ds(0, n - 1)]
+        pltpu.make_async_copy(every, every, send_sem.at[phase]).wait()
+
     column = iota((blocks, 128), 1)
-    item = (column // 2) % blocks
+    item = (column >> 1) % blocks
     block = iota((blocks, 128), 0)
-    here = [jnp.broadcast_to(mine[:, v : v + 1], (blocks, 128)) for v in range(VES)]
+    length = dest_ref.shape[1]
+    wanted = iota((blocks, length), 1) - iota((blocks, length), 0) == me * blocks
+    here = [
+        jnp.broadcast_to(
+            jnp.sum(jnp.where(wanted, dest_ref[v : v + 1], 0), axis=1, keepdims=True), (blocks, 128)
+        )
+        for v in range(VES)
+    ]
     lane = iota((1, 128), 1)
-    inner = (lane % 2) * 4 + lane // 32
+    inner = (lane & 1) * 4 + (lane >> 5)
     rows = iota((16 * n, 128), 0)
     mask = None
     for v in range(VES):
@@ -117,17 +120,17 @@
     k = iota((36, 256), 1)
     for q in range(4):
         span = slice(64 * q, 64 * q + 64)
-        wt1[span] = dot(w_in_ref[...], onehot(u == tap_of(k, q, False)).astype(BF16)).astype(BF16)
-        wt2[span] = dot(w_out_ref[...], onehot(u == tap_of(k, q, True)).astype(BF16)).astype(BF16)
+        wt1[span] = dot(w_in_ref[...], onehot(u == tap_of(k, q, False)).astype(BF16), TN).astype(BF16)
+        wt2[span] = dot(w_out_ref[...], onehot(u == tap_of(k, q, True)).astype(BF16), TN).astype(BF16)
     wt2_t[...] = wt2[...].astype(F32).T.astype(BF16)
-    tall = onehot(iota((256, 64), 0) % 64 == iota((256, 64), 1)).astype(BF16)
-    wide = onehot(iota((64, 256), 1) % 64 == iota((64, 256), 0)).astype(BF16)
-    diagonal = iota((256, 256), 0) // 64 == iota((256, 256), 1) // 64
+    tall = onehot((iota((256, 64), 0) & 63) == iota((256, 64), 1)).astype(BF16)
+    wide = onehot((iota((64, 256), 1) & 63) == iota((64, 256), 0)).astype(BF16)
+    diagonal = iota((256, 256), 0) >> 6 == iota((256, 256), 1) >> 6
     once = dot(dot(tall, w_mid_ref[...]).astype(BF16), wide)
     once = jnp.where(diagonal, once, 0.0)
     wm[...] = once.astype(BF16)
     wm_t[...] = once.T.astype(BF16)
-    near = iota((256, 64), 0) % 64 == iota((256, 64), 1)
+    near = (iota((256, 64), 0) & 63) == iota((256, 64), 1)
     for b_ref, bias in ((b_in_ref, bias1), (b_mid_ref, bias2)):
         values = jnp.sum(jnp.where(near, b_ref[...], 0.0), axis=1, keepdims=True)
         bias[...] = jnp.broadcast_to(values, (256, 128))
@@ -156,7 +159,7 @@
                 field[32:48, at] = moved[span, 128:256]
             return 0
 
-        lax.fori_loop(0, n // 8, step, 0)
+        lax.fori_loop(0, n // 8, step, 0, unroll=4)
 
     size = chunk * 128
 
@@ -199,8 +202,16 @@
         est[s] = (acc[16:32, at] + before + after).astype(BF16)
         return 0
 
-    lax.fori_loop(0, n, close, 0)
+    lax.fori_loop(0, n, close, 0, unroll=8)
     exchange(est, in2, 1)
+    deep = iota((256, 128), 0)
+    across = iota((256, 128), 1)
+    for q in range(4):
+        tap = tap_of(deep, q, True)
+        fold1[q] = onehot(
+            (across == tap_of(deep, q, False)) | ((deep == 112) & (across == 36))
+        ).astype(BF16)
+        fold2[q] = onehot((across - 64 == tap) & (tap >= 0)).astype(BF16)
     arrive(in2, 1)
     residual = dot(sel_t[...], in2[...].reshape(16 * n, 128)) - rec_ref[...].astype(F32)
     res_ref[...] = residual
@@ -225,21 +236,16 @@
     lax.fori_loop(0, n // chunk, backward, 0)
 
     lane = iota((64, 128), 1)
-    deep = iota((256, 128), 0)
-    across = iota((256, 128), 1)
     first = jnp.zeros((64, 128), F32)
     for q in range(4):
         span = slice(64 * q, 64 * q + 64)
-        for g, fold in (
-            (g1, (across == tap_of(deep, q, False)) | ((deep == 112) & (across == 36))),
-            (g2, across - 64 == jnp.where(tap_of(deep, q, True) < 0, -100, tap_of(deep, q, True))),
-        ):
+        for g, fold in ((g1, fold1), (g2, fold2)):
             x = g[span]
             high = x.astype(BF16)
             rest = x - high.astype(F32)
             middle = rest.astype(BF16)
             low = (rest - middle.astype(F32)).astype(BF16)
-            three = dot(jnp.concatenate([high, middle, low], axis=0), onehot(fold).astype(BF16))
+            three = dot(jnp.concatenate([high, middle, low], axis=0), fold[q])
             first = first + (three[0:64] + three[64:128] + three[128:192])
     square = jnp.where(diagonal, gm[...], 0.0)
     square = square[0:64] + square[64:128] + square[128:192] + square[192:256]
@@ -247,12 +253,13 @@
     square = square + pltpu.roll(square, 64, 1)
     summed = jnp.sum(gb[...], axis=1, keepdims=True)
     summed = summed[0:64] + summed[64:128] + summed[128:192] + summed[192:256]
-    second = jnp.where(lane < 64, square, jnp.where(lane == 64, summed, 0.0))
+    first = jnp.where(lane == 37, summed, first)
+    first = jnp.concatenate([first, jnp.zeros((64, 128), F32)], axis=0).T
+    total = [first[0:64] + jnp.where(lane >= 64, square, 0.0), first[64:128]]
     per = 128 // n
     for i in range(n):
-        source = first if i * per < 64 else second
         start = (i * per) % 64
-        parts[i] = source[start : start + per]
+        parts[i] = total[i * per // 64][start : start + per]
 
     exchange(parts, in4, 3)
     arrive(in4, 3)
@@ -270,7 +277,7 @@
         ).start()
         return 0
 
-    lax.fori_loop(1, n, share, 0)
+    lax.fori_loop(1, n, share, 0, unroll=True)
     in5[me] = part[0]
     arrive(in5, 4)
     for i in range(n):
@@ -280,6 +287,15 @@
     sent(out3, 2)
     sent(parts, 3)
     sent(in5, 4)
+
+
+def deal(res_ref, grad_ref, out_ref, dwi_ref, dbi_ref, dwm_ref, dbm_ref, dwo_ref):
+    out_ref[...] = res_ref[...]
+    dwi_ref[...] = grad_ref[0:36, 0:64]
+    dbi_ref[...] = grad_ref[36:37, 0:64]
+    dbm_ref[...] = grad_ref[37:38, 0:64]
+    dwo_ref[...] = grad_ref[64:100, 0:64]
+    dwm_ref[...] = pltpu.roll(grad_ref[0:64], 64, 1)[:, 0:64]
 
 
 def local(n, records, dest, w_in, b_in, w_mid, b_mid, w_out):
@@ -292,16 +308,15 @@
     V = pltpu.VMEM
     message = V((n, 16, 128), BF16)
     piece = V((n, per, 128), F32)
-    residual, grads = pl.pallas_call(
+    result = pl.pallas_call(
         functools.partial(kernel, n, scale, chunk),
         out_shape=(
             jax.ShapeDtypeStruct((128, 128), F32),
             jax.ShapeDtypeStruct((128, 128), F32),
         ),
-        in_specs=[vmem, pl.BlockSpec(memory_space=pl.ANY)] + [vmem] * 5,
-        out_specs=(vmem, vmem),
+        in_specs=[vmem] * 7,
+        out_specs=(vmem,) * 2,
         scratch_shapes=[
-            V((blocks, VES), jnp.int32),
             message, message, message, message, message, message,
             piece, piece, V((1, per, 128), F32), piece,
             V((16 * n, 128), BF16), V((128, 16 * n), BF16),
@@ -311,22 +326,37 @@
             V((64, width + 256), BF16), V((64, width + 256), BF16), V((48, width + 256), F32),
             V((256, width), BF16), V((256, width), BF16), V((256, width), F32), V((256, width), F32),
             V((256, 256), F32), V((256, 256), F32), V((256, 256), F32), V((256, 128), F32),
-            pltpu.SemaphoreType.DMA, pltpu.SemaphoreType.DMA((5,)), pltpu.SemaphoreType.DMA((5,)),
+            V((4, 256, 128), BF16), V((4, 256, 128), BF16),
+            pltpu.SemaphoreType.DMA((5,)), pltpu.SemaphoreType.DMA((5,)),
         ],
         compiler_params=pltpu.CompilerParams(
-            collective_id=0, has_side_effects=True, vmem_limit_bytes=63 * 1024 * 1024
+            collective_id=0, has_side_effects=True, vmem_limit_bytes=63 << 20
         ),
         name="deblend",
     )(
-        records.reshape(128, 128), dest, w_in, b_in.reshape(1, 64), w_mid, b_mid.reshape(1, 64), w_out
+        records.reshape(128, 128), dest.T, w_in.T, b_in.reshape(1, 64), w_mid, b_mid.reshape(1, 64), w_out.T
     )
+    residual, dwi, dbi, dwm, dbm, dwo = pl.pallas_call(
+        deal,
+        out_shape=(
+            jax.ShapeDtypeStruct((128, 128), F32),
+            jax.ShapeDtypeStruct((36, 64), F32),
+            jax.ShapeDtypeStruct((1, 64), F32),
+            jax.ShapeDtypeStruct((64, 64), F32),
+            jax.ShapeDtypeStruct((1, 64), F32),
+            jax.ShapeDtypeStruct((36, 64), F32),
+        ),
+        in_specs=[vmem] * 2,
+        out_specs=(vmem,) * 6,
+        name="deal",
+    )(*result)
     return (
         residual.reshape(records.shape),
-        grads[0:64, 0:36],
-        grads[0:64, 36],
-        grads[64:128, 0:64],
-        grads[64:128, 64],
-        grads[0:64, 64:100],
+        dwi.T,
+        dbi.reshape(64),
+        dwm,
+        dbm.reshape(64),
+        dwo.T,
     )
 
 

time: 58.2 us -> 49.1 us (0.84)
  local copies, waits for them, and re-layouts: 7.2 us -> 0 us
  Pallas kernels: 49.9 us -> 48.3 us
    unnamed x14 -> x0, local copies, waits for them, and re-layouts: 4.97 us -> none
    pallas_call x1, Pallas kernels: 49.9 us -> 46.7 us  [local(): pl.pallas_call(functools.partial(kernel, n, scale, chunk), out_shape=(jax...]
    slice x3 -> x0, local copies, waits for them, and re-layouts: 2.23 us -> none  [the longest x1 1.53 us: local(): grads[64:128, 64]]
    pallas_call x0 -> x1, Pallas kernels: none -> 1.57 us  [local(): pl.pallas_call(deal, out_shape=(jax.ShapeDtypeStruct((128, 128), F32), ja...]
where the time goes in v2:
time: 49.1 us; the launch traced here: 48.9 us
  Pallas kernels  48.3 us (98%)
  between operations  0.64 us (1%)
    pallas_call x1, Pallas kernels, local(): pl.pallas_call(functools.partial(kernel, n, scale, chunk), out_shape=(jax...  46.7 us
    pallas_call x1, Pallas kernels, local(): pl.pallas_call(deal, out_shape=(jax.ShapeDtypeStruct((128, 128), F32), ja...  1.57 us

profile of v2, /device:TPU:0, one launch (start us, length us, event | category | flops | bytes accessed | tf_op | source)
XLA Modules:
  0.0 48.9 jit_solution(5165783130797224933)
XLA Ops:
  0.6 46.7 %deblend.1 = (f32[128,128]{1,0:T(8,128)}, f32[128,128]{1,0:T(8,128)}) custom-call(bf16[128,128]{1,0:T(8,128)(2,1)} %bitcast.11, s32[4,512]{1,0:T(4,128)} %bitcast.14, bf16[36,64]{1,0:T(8,128)(2,1)} %bitcast.12, f32[1,64]{1,0:T(1,128)} %bitcast.15, bf16[64,64]{1,0:T(8,128)(2,1)} %w_mid_ref.1, f32[1,64]{1,0:T(1,128)} %bitcast.16, bf16[36,64]{1,0:T(8,128)(2,1)} %bitcast.13), custom_call_target="tpu_custom_call" | custom-call | tf_op jit(solution)/shard_map/deblend/pallas_call | solution.py:311
  47.3 1.6 %deal.1 = (f32[128,128]{1,0:T(8,128)}, f32[36,64]{1,0:T(8,128)}, f32[1,64]{1,0:T(1,128)}, f32[64,64]{1,0:T(8,128)}, f32[1,64]{1,0:T(1,128)}, /*index=5*/f32[36,64]{1,0:T(8,128)}) custom-call(f32[128,128]{1,0:T(8,128)} %get-tuple-element.14.res_ref, f32[128,128]{1,0:T(8,128)} %get-tuple-element.15.grad_ref), custom_call_target="tpu_custom_call" | custom-call | tf_op jit(solution)/shard_map/deal/pallas_call | solution.py:339

commit v3 on v2

--- a/solution.py
+++ b/solution.py
@@ -302,7 +302,7 @@
     parts, blocks, traces, samples = records.shape
     width = n * samples
     per = 128 // n
-    chunk = 4
+    chunk = max(4, 512 // n)
     scale = 1.0 / math.sqrt(parts * blocks * n * traces * samples)
     vmem = pl.BlockSpec(memory_space=pltpu.VMEM)
     V = pltpu.VMEM

time: 49.1 us -> 45.5 us (0.927)
  Pallas kernels: 48.3 us -> 44.6 us
    pallas_call x1, Pallas kernels: 46.7 us -> 43 us  [local(): pl.pallas_call(functools.partial(kernel, n, scale, chunk), out_shape=(jax...]
where the time goes in v3:
time: 45.5 us; the launch traced here: 45.2 us
  Pallas kernels  44.6 us (98%)
  between operations  0.64 us (1%)
    pallas_call x1, Pallas kernels, local(): pl.pallas_call(functools.partial(kernel, n, scale, chunk), out_shape=(jax...  43 us
    pallas_call x1, Pallas kernels, local(): pl.pallas_call(deal, out_shape=(jax.ShapeDtypeStruct((128, 128), F32), ja...  1.57 us

profile of v3, /device:TPU:0, one launch (start us, length us, event | category | flops | bytes accessed | tf_op | source)
XLA Modules:
  0.0 45.2 jit_solution(12170435769975993737)
XLA Ops:
  0.6 43.0 %deblend.1 = (f32[128,128]{1,0:T(8,128)}, f32[128,128]{1,0:T(8,128)}) custom-call(bf16[128,128]{1,0:T(8,128)(2,1)} %bitcast.11, s32[4,512]{1,0:T(4,128)} %bitcast.14, bf16[36,64]{1,0:T(8,128)(2,1)} %bitcast.12, f32[1,64]{1,0:T(1,128)} %bitcast.15, bf16[64,64]{1,0:T(8,128)(2,1)} %w_mid_ref.1, f32[1,64]{1,0:T(1,128)} %bitcast.16, bf16[36,64]{1,0:T(8,128)(2,1)} %bitcast.13), custom_call_target="tpu_custom_call" | custom-call | tf_op jit(solution)/shard_map/deblend/pallas_call | solution.py:311
  43.7 1.6 %deal.1 = (f32[128,128]{1,0:T(8,128)}, f32[36,64]{1,0:T(8,128)}, f32[1,64]{1,0:T(1,128)}, f32[64,64]{1,0:T(8,128)}, f32[1,64]{1,0:T(1,128)}, /*index=5*/f32[36,64]{1,0:T(8,128)}) custom-call(f32[128,128]{1,0:T(8,128)} %get-tuple-element.14.res_ref, f32[128,128]{1,0:T(8,128)} %get-tuple-element.15.grad_ref), custom_call_target="tpu_custom_call" | custom-call | tf_op jit(solution)/shard_map/deal/pallas_call | solution.py:339
